TPU v7x, 32 devices: a whole 2x2x4 slice. The times are simulated.
32 devices in a mesh: groups: 1, ex: 32 (over z, y, x, core).
Axes of the slice: x: 2, y: 2, z: 4, core: 2. Of those that a mesh axis runs over, the one named last changes fastest.
Arguments:
- residual_in: bfloat16 [2, 1024, 2048], P(None, ('groups', 'ex')), may hold values from -6 to 6
- queries: bfloat16 [2, 1024, 2048], P(None, ('groups', 'ex')), may hold values from -100 to 100
- new_entries: bfloat16 [2, 1024, 2, 256], P(None, ('groups', 'ex')), may hold values from -6 to 6
- cache_keys: bfloat16 [2, 1024, 64, 256], P(None, ('groups', 'ex')), may hold values from -4.5 to 4.5
- cache_values: bfloat16 [2, 1024, 64, 256], P(None, ('groups', 'ex')), may hold values from -6 to 6
- lengths: int32 [2, 1024], P(None, ('groups', 'ex')), may hold values from 2 to 64, as said below
- skip_flags: int32 [2, 1024], P(None, ('groups', 'ex')), may hold values 0 or 1
- expert_ids: int32 [2, 1024, 8], P(None, ('groups', 'ex')), may hold values from 0 to 31, all different within a row; in each aligned block of 32 rows (0 to 31, 32 to 63, ..., all dimensions but the last counted through in order) at most 16 rows name the same one
- gate_weights: float32 [2, 1024, 8], P(None, ('groups', 'ex')), may hold values from 0.1 to 1
- norm_gain: float32 [2048], replicated, may hold values from 0.1 to 1.9
- gate_proj: bfloat16 [32, 2048, 768], P('ex'), may hold values from -0.125 to 0.125
- up_proj: bfloat16 [32, 2048, 768], P('ex'), may hold values from -0.125 to 0.125
- down_proj: bfloat16 [32, 768, 2048], P('ex'), may hold values from -0.21875 to 0.21875
Outputs:
- layer_out: bfloat16 [2, 1024, 2048], P(None, ('groups', 'ex'))
Inputs may be any that keep to these rules, and one draw needn't show every extreme that they name: `expert_ids`: in each micro-batch, the 32 rows of one device name any one expert at most 16 times; each row names 8 different experts. `lengths`: in each micro-batch, every device's block of 32 rows holds a row of length 64.
All inputs are finite; a program needn't handle non-finite values. No bound on the sum of `skip_flags` on one device may be relied on, other than what follows from the above.
Results may differ from a plain program's by a relative error of at most 0.0065.
Values may be sent and summed in bfloat16 or wider, within the bound.
A program may use at most 128 MiB of HBM per device.

v0:
```python
import jax
import jax.numpy as jnp
from jax import lax
from jax.sharding import PartitionSpec as P

HEADS = 16
KEY_VALUE_HEADS = 2
HEAD_WIDTH = 128


def attend(queries, entries, keys, value_entries, lengths):
    token_row_count = queries.shape[0]
    cache_slot_index = keys.shape[1]
    group = HEADS // KEY_VALUE_HEADS
    scale = HEAD_WIDTH ** (-0.5)
    qvec = queries.reshape(token_row_count, KEY_VALUE_HEADS, group, HEAD_WIDTH)
    kmat = keys.reshape(token_row_count, cache_slot_index, KEY_VALUE_HEADS, HEAD_WIDTH)
    value_matrix = value_entries.reshape(
        token_row_count, cache_slot_index, KEY_VALUE_HEADS, HEAD_WIDTH
    )
    own_key = entries[:, 0].reshape(token_row_count, KEY_VALUE_HEADS, HEAD_WIDTH)
    self_value_vector = entries[:, 1].reshape(token_row_count, KEY_VALUE_HEADS, HEAD_WIDTH)
    cache_scores = (
        jnp.einsum("rkgd,rlkd->rkgl", qvec, kmat, preferred_element_type=jnp.float32) * scale
    )
    own_scores = (
        jnp.einsum("rkgd,rkd->rkg", qvec, own_key, preferred_element_type=jnp.float32) * scale
    )
    live = (jnp.arange(cache_slot_index, dtype=jnp.int32)[None, :] < lengths[:, None])[
        :, None, None, :
    ]
    cache_scores = jnp.where(live, cache_scores, -1e30)
    top = jnp.maximum(jnp.max(cache_scores, axis=-1), own_scores)
    cache_p = jnp.where(live, jnp.exp(cache_scores - top[..., None]), 0.0)
    own_p = jnp.exp(own_scores - top)
    total = jnp.sum(cache_p, axis=-1) + own_p
    cache_weight_part = (cache_p / total[..., None]).astype(jnp.bfloat16)
    self_weight_part = (own_p / total).astype(jnp.bfloat16)
    blended_output = jnp.einsum(
        "xtio,xotw->xtiw", cache_weight_part, value_matrix, preferred_element_type=jnp.float32
    )
    blended_output = blended_output + self_weight_part[..., None].astype(
        jnp.float32
    ) * self_value_vector[:, :, None, :].astype(jnp.float32)
    return blended_output.reshape(token_row_count, HEADS * HEAD_WIDTH).astype(jnp.bfloat16)


def prepare(residual, queries, entries, keys, value_entries, lengths, norm_gain):
    attended = attend(queries, entries, keys, value_entries, lengths)
    stream = residual.astype(jnp.float32) + attended.astype(jnp.float32)
    meansq = jnp.mean(stream * stream, axis=-1, keepdims=True)
    normed = (stream / jnp.sqrt(meansq + 1e-06) * norm_gain[None, :]).astype(jnp.bfloat16)
    return (stream, normed)


def combine_table(expert_ids, gate_weights, experts):
    gates = gate_weights / jnp.sum(gate_weights, axis=-1, keepdims=True)
    named = expert_ids[..., None] == jnp.arange(experts, dtype=jnp.int32)
    return jnp.sum(jnp.where(named, gates[..., None], 0.0), axis=-2)


def expert_rows(flat, gate_proj, up_proj, down_proj):
    gate = jnp.dot(flat, gate_proj[0], preferred_element_type=jnp.float32)
    upper = jnp.dot(flat, up_proj[0], preferred_element_type=jnp.float32)
    hidden = (jax.nn.silu(gate) * upper).astype(jnp.bfloat16)
    return jnp.dot(hidden, down_proj[0], preferred_element_type=jnp.float32).astype(jnp.bfloat16)


def on_device(
    residual_in,
    queries,
    new_entries,
    cache_keys,
    cache_values,
    lengths,
    skip_flags,
    expert_ids,
    gate_weights,
    norm_gain,
    gate_proj,
    up_proj,
    down_proj,
):
    micro_count, rows, width = residual_in.shape
    shards = lax.axis_size("ex")
    experts = gate_proj.shape[0] * shards
    table = combine_table(expert_ids, gate_weights, experts)
    mine = lax.all_to_all(table, "ex", split_axis=2, concat_axis=1, tiled=True)
    results = []
    for micro in range(micro_count):
        stream, normed = prepare(
            residual_in[micro],
            queries[micro],
            new_entries[micro],
            cache_keys[micro],
            cache_values[micro],
            lengths[micro],
            norm_gain,
        )
        gathered = lax.all_gather(normed, "ex", axis=0, tiled=True)
        out = expert_rows(gathered, gate_proj, up_proj, down_proj)
        partial = (mine[micro] * out.astype(jnp.float32)).astype(jnp.bfloat16)
        mixture = lax.psum_scatter(partial, "ex", scatter_dimension=0, tiled=True)
        merged = (stream + mixture.astype(jnp.float32)).astype(jnp.bfloat16)
        results.append(jnp.where(skip_flags[micro][:, None] == 1, residual_in[micro], merged))
    return jnp.stack(results, axis=0)


def solution(mesh):
    in_specs = (
        P(None, ("groups", "ex"), None),
        P(None, ("groups", "ex"), None),
        P(None, ("groups", "ex"), None, None),
        P(None, ("groups", "ex"), None, None),
        P(None, ("groups", "ex"), None, None),
        P(None, ("groups", "ex")),
        P(None, ("groups", "ex")),
        P(None, ("groups", "ex"), None),
        P(None, ("groups", "ex"), None),
        P(),
        P("ex", None, None),
        P("ex", None, None),
        P("ex", None, None),
    )
    out_specs = P(None, ("groups", "ex"), None)
    return jax.shard_map(
        on_device, mesh=mesh, in_specs=in_specs, out_specs=out_specs, check_vma=False
    )
```

profile of v0, /device:TPU:0, one launch (start us, length us, event | category | flops | bytes accessed | tf_op | source)
XLA Modules:
  0.0 465.2 jit_solution(1728249540020639107)
XLA Ops:
  7.4 1.8 slice_bitcast_fusion.1
  9.2 3.1 fusion.54
  12.3 2.2 reshape_squeeze.29
  14.5 2.6 fusion.57
  17.9 1.4 slice_bitcast_fusion.5
  23.5 1.5 slice_convert_fusion
  24.9 3.1 fusion.55
  28.0 2.2 reshape_squeeze.31
  31.1 2.1 reshape_squeeze.25
  33.3 1.6 fusion.42
  34.9 3.2 fusion.56
  39.8 1.2 fusion.28
  41.3 2.1 reshape_squeeze.27
  43.5 1.8 fusion.19
  48.9 14.3 %all_to_all.15 = f32[2,32,32]{1,0,2:T(2,128)S(1)} all-to-all(f32[2,32,32]{1,0,2:T(2,128)S(1)} %copy.57), channel_id=1, replica_groups=mesh['groups'=1,'ex'=32] {'ex'}, dimensions={2} | all-to-all | bytes 16384 | tf_op jit(solution)/shard_map/all_to_all | solution.py:88
  63.4 49.0 %all-gather.5.cloned.1.call-done = bf16[1024,2048]{1,0:T(8,128)(2,1)} async-done(((bf16[32,2048]{1,0:T(8,128)(2,1)}), bf16[1024,2048]{1,0:T(8,128)(2,1)}) %all-gather.5.cloned.1.call-update) | async-done | bytes 4194320 | tf_op jit(solution)/shard_map/all_gather | solution.py:100
  112.4 8.2 %fusion.2 = f32[1024,768]{1,0:T(8,128)} fusion(bf16[1024,2048]{1,0:T(8,128)(2,1)} %all-gather.5.cloned.1.call-done, bf16[1,2048,768]{2,1,0:T(8,128)(2,1)} %param.24), kind=kOutput, calls=%fused_computation.4 | convolution fusion | flops 3221225472 | bytes 10485760 | tf_op jit(solution)/shard_map/dot_general | solution.py:64
  120.6 12.5 %multiply_convert_fusion = bf16[1024,2048]{1,0:T(8,128)(2,1)} fusion(f32[1024]{0:T(1024)S(1)} %mul.109, bf16[1,768,2048]{2,1,0:T(8,128)(2,1)S(1)} %copy-done, f32[1024,768]{1,0:T(8,128)} %fusion.2, bf16[1024,2048]{1,0:T(8,128)(2,1)} %all-gather.5.cloned.1.call-done, bf16[1,2048,768]{2,1,0:T(8,128)(2,1)} %param.23), kind=kOutput, calls=%fused_computation | convolution fusion | flops 6455558144 | bytes 17829888 | tf_op jit(solution)/shard_map/dot_general | solution.py:66
  133.4 42.5 %all-gather.3.cloned.1.call-done = bf16[1024,2048]{1,0:T(8,128)(2,1)} async-done(((bf16[32,2048]{1,0:T(8,128)(2,1)}), bf16[1024,2048]{1,0:T(8,128)(2,1)}) %all-gather.3.cloned.1.call-update) | async-done | bytes 4194320 | tf_op jit(solution)/shard_map/all_gather | solution.py:100
  175.9 8.2 %fusion.4 = f32[1024,768]{1,0:T(8,128)} fusion(bf16[1024,2048]{1,0:T(8,128)(2,1)} %all-gather.3.cloned.1.call-done, bf16[1,2048,768]{2,1,0:T(8,128)(2,1)} %param.24), kind=kOutput, calls=%fused_computation.6 | convolution fusion | flops 3221225472 | bytes 10485760 | tf_op jit(solution)/shard_map/dot_general | solution.py:64
  184.1 12.3 %multiply_convert_fusion.1 = bf16[1024,2048]{1,0:T(8,128)(2,1)} fusion(f32[1024]{0:T(1024)S(1)} %mul.96, bf16[1,768,2048]{2,1,0:T(8,128)(2,1)S(1)} %copy-done, f32[1024,768]{1,0:T(8,128)} %fusion.4, bf16[1024,2048]{1,0:T(8,128)(2,1)} %all-gather.3.cloned.1.call-done, bf16[1,2048,768]{2,1,0:T(8,128)(2,1)} %param.23), kind=kOutput, calls=%fused_computation.1 | convolution fusion | flops 6455558144 | bytes 17829888 | tf_op jit(solution)/shard_map/dot_general | solution.py:66
  197.1 120.5 %reduce-scatter.5.cloned.1.call-done = bf16[32,2048]{1,0:T(8,128)(2,1)} async-done(((bf16[1024,2048]{1,0:T(8,128)(2,1)}), bf16[32,2048]{1,0:T(8,128)(2,1)}) %reduce-scatter.5.cloned.1.call-update) | async-done | bytes 131088 | tf_op jit(solution)/shard_map/reduce_scatter | solution.py:103
  317.6 139.0 %reduce-scatter.3.cloned.1.call-done = bf16[32,2048]{1,0:T(8,128)(2,1)} async-done(((bf16[1024,2048]{1,0:T(8,128)(2,1)}), bf16[32,2048]{1,0:T(8,128)(2,1)}) %reduce-scatter.3.cloned.1.call-update) | async-done | bytes 131088 | tf_op jit(solution)/shard_map/reduce_scatter | solution.py:103
  456.6 2.1 fusion.31
  (72 shorter events, 13.3 us)
Async XLA Ops:
  6.5 114.1 %copy-start = (bf16[1,768,2048]{2,1,0:T(8,128)(2,1)S(1)}, bf16[1,768,2048]{2,1,0:T(8,128)(2,1)}, u32[]{:S(2)}) copy-start(bf16[1,768,2048]{2,1,0:T(8,128)(2,1)} %param.25) | copy-start | bytes 9437188
  6.5 105.9 %all-gather.5.cloned.1.call-start = ((), (), s32[]{:S(2)}) async-start(), calls=%async_computation.5 | async-start | bytes 4325376 | tf_op jit(solution)/shard_map/all_gather | solution.py:100
  19.4 0.6 copy-start.6
  21.7 8.5 %copy-start.7 = (f32[32,2,8]{2,1,0:T(2,128)}, f32[32,2,8]{2,1,0:T(2,128)S(1)}, u32[]{:S(2)}) copy-start(f32[32,2,8]{2,1,0:T(2,128)S(1)} %copy.60) | copy-start | bytes 6148
  43.5 1.9 copy-start.4
  43.5 1.9 copy-start.5
  43.5 1.9 copy-start.9
  45.3 1.3 copy-start.2
  45.3 1.0 copy-start.1
  45.4 1.3 copy-start.10
  45.4 3.0 copy-start.8
  45.4 3.1 copy-start.11
  45.8 1.7 copy-start.3
  47.6 128.3 %all-gather.3.cloned.1.call-start = ((), (), s32[]{:S(2)}) async-start(), calls=%async_computation.3 | async-start | bytes 4325376 | tf_op jit(solution)/shard_map/all_gather | solution.py:100
  48.3 269.3 %reduce-scatter.5.cloned.1.call-start = ((), (), s32[]{:S(2)}) async-start(), calls=%async_computation.6 | async-start | bytes 4325376 | tf_op jit(solution)/shard_map/reduce_scatter | solution.py:103
  133.1 323.5 %reduce-scatter.3.cloned.1.call-start = ((), (), s32[]{:S(2)}) async-start(), calls=%async_computation.4 | async-start | bytes 4325376 | tf_op jit(solution)/shard_map/reduce_scatter | solution.py:103
  196.4 0.7 copy-start.12
Sparse Core Ops, SparseCore 0:
  47.7 64.6 all-gather.4
  115.3 60.5 all-gather.2
  178.2 139.4 reduce-scatter.4
  319.8 136.7 reduce-scatter.2
where the time goes:
time: 466 us; the launch traced here: 465 us
  waiting for transfers between devices  352 us (76%)
  matrix products  51.6 us (11%)
  local copies, waits for them, and re-layouts  27.3 us (6%)
  blocking collectives  14.3 us (3%)
  between operations  13.3 us (3%)
  other arithmetic  6.58 us (1%)
    reduce_scatter x2, waiting for transfers between devices, on_device(): mixture = lax.psum_scatter(partial, 'ex', scatter_dimension=0, tiled=True)  260 us
    all_gather x2, waiting for transfers between devices, on_device(): gathered = lax.all_gather(normed, 'ex', axis=0, tiled=True)  91.5 us
    dot_general x2, matrix products, expert_rows(): jnp.dot(hidden, down_proj[0], preferred_element_type=jnp.float32)  24.8 us
    dot_general x2, matrix products, expert_rows(): upper = jnp.dot(flat, up_proj[0], preferred_element_type=jnp.float32)  16.4 us
    all_to_all x1, blocking collectives, on_device(): mine = lax.all_to_all(table, 'ex', split_axis=2, concat_axis=1, tiled=True)  14.3 us
  transfers between devices with their start and end apart: 4, of which 4 were waited for; matrix products, arithmetic and copies ran while one was open for 9% of the time, Pallas kernels for 0%

commit v1 on v0

--- a/solution.py
+++ b/solution.py
@@ -97,7 +97,19 @@
             lengths[micro],
             norm_gain,
         )
-        gathered = lax.all_gather(normed, "ex", axis=0, tiled=True)
+        work_now = lax.axis_size("ex")
+        later = lax.axis_index("ex")
+        kept_arr, x_now = (work_now, later)
+        gathered, block_out = (normed, 1)
+        while block_out < kept_arr:
+            made = []
+            for k in range(kept_arr):
+                made.append((k, k ^ block_out))
+            reply = lax.ppermute(gathered, axis_name="ex", perm=made)
+            u1 = jnp.concatenate([gathered, reply], axis=0)
+            y2 = jnp.concatenate([reply, gathered], axis=0)
+            gathered = jnp.where(x_now & block_out == 0, u1, y2)
+            block_out = 2 * block_out
         out = expert_rows(gathered, gate_proj, up_proj, down_proj)
         partial = (mine[micro] * out.astype(jnp.float32)).astype(jnp.bfloat16)
         mixture = lax.psum_scatter(partial, "ex", scatter_dimension=0, tiled=True)

time: 466 us -> 566 us (1.21)
  waiting for transfers between devices: 352 us -> 415 us
  starting transfers between devices: 0.3 us -> 20 us
  other arithmetic: 6.58 us -> 23.7 us
  blocking collectives: 14.3 us -> 0 us
  matrix products: 51.6 us -> 58.8 us
  local copies, waits for them, and re-layouts: 27.3 us -> 33.4 us
    ppermute x0 -> x10, waiting for transfers between devices: none -> 193 us  [on_device(): reply = lax.ppermute(gathered, axis_name='ex', perm=made)]
    reduce_scatter x2, waiting for transfers between devices: 260 us -> 141 us  [on_device(): mixture = lax.psum_scatter(partial, 'ex', scatter_dimension=0, tiled=True)]
    all_gather x2 -> x0, waiting for transfers between devices: 91.5 us -> none  [on_device(): gathered = lax.all_gather(normed, 'ex', axis=0, tiled=True)]
    all_to_all x0 -> x1, waiting for transfers between devices: none -> 80.5 us  [on_device(): mine = lax.all_to_all(table, 'ex', split_axis=2, concat_axis=1, tiled=True)]
    ppermute x0 -> x10, starting transfers between devices: none -> 15.6 us  [on_device(): reply = lax.ppermute(gathered, axis_name='ex', perm=made)]
    select_n x0 -> x8, other arithmetic: none -> 14.6 us  [on_device(): gathered = jnp.where(x_now & block_out == 0, u1, y2)]
    all_to_all x1 -> x0, blocking collectives: 14.3 us -> none  [on_device(): mine = lax.all_to_all(table, 'ex', split_axis=2, concat_axis=1, tiled=True)]
  transfers between devices with their start and end apart: 4 -> 13, of which waited for: 4 -> 11; matrix products, arithmetic and copies ran while one was open for 9% -> 6% of each run, Pallas kernels for 0% -> 0%
where the time goes in v1:
time: 566 us; the launch traced here: 564 us
  waiting for transfers between devices  415 us (73%)
  matrix products  58.8 us (10%)
  local copies, waits for them, and re-layouts  33.4 us (6%)
  other arithmetic  23.7 us (4%)
  starting transfers between devices  20 us (4%)
  between operations  13.6 us (2%)
    ppermute x10, waiting for transfers between devices, on_device(): reply = lax.ppermute(gathered, axis_name='ex', perm=made)  193 us
    reduce_scatter x2, waiting for transfers between devices, on_device(): mixture = lax.psum_scatter(partial, 'ex', scatter_dimension=0, tiled=True)  141 us
    all_to_all x1, waiting for transfers between devices, on_device(): mine = lax.all_to_all(table, 'ex', split_axis=2, concat_axis=1, tiled=True)  80.5 us
    dot_general x2, matrix products, expert_rows(): jnp.dot(hidden, down_proj[0], preferred_element_type=jnp.float32)  29.2 us
    dot_general x2, matrix products, expert_rows(): upper = jnp.dot(flat, up_proj[0], preferred_element_type=jnp.float32)  19.1 us
    ppermute x10, starting transfers between devices, on_device(): reply = lax.ppermute(gathered, axis_name='ex', perm=made)  15.6 us
    select_n x8, other arithmetic, on_device(): gathered = jnp.where(x_now & block_out == 0, u1, y2)  14.6 us
  transfers between devices with their start and end apart: 13, of which 11 were waited for; matrix products, arithmetic and copies ran while one was open for 6% of the time, Pallas kernels for 0%

profile of v1, /device:TPU:0, one launch (start us, length us, event | category | flops | bytes accessed | tf_op | source)
XLA Modules:
  0.0 564.1 jit_solution(3559660128534547133)
XLA Ops:
  9.2 3.1 fusion.62
  14.5 2.6 fusion.65
  25.0 3.1 fusion.63
  28.1 2.2 reshape_squeeze.31
  35.0 3.2 fusion.64
  51.3 2.8 collective-permute-start.6
  54.1 6.9 %collective-permute-done.6 = bf16[64,2048]{1,0:T(8,128)(2,1)} collective-permute-done((bf16[64,2048]{1,0:T(8,128)(2,1)}, bf16[64,2048]{1,0:T(8,128)(2,1)}, u32[]{:S(2)}, u32[]{:S(2)}) %collective-permute-start.6) | collective-permute-done | bytes 262176 | tf_op jit(solution)/shard_map/ppermute | solution.py:108
  65.0 12.0 %collective-permute-done.7 = bf16[128,2048]{1,0:T(8,128)(2,1)} collective-permute-done((bf16[128,2048]{1,0:T(8,128)(2,1)}, bf16[128,2048]{1,0:T(8,128)(2,1)}, u32[]{:S(2)}, u32[]{:S(2)}) %collective-permute-start.7) | collective-permute-done | bytes 524320 | tf_op jit(solution)/shard_map/ppermute | solution.py:108
  77.0 2.9 maximum_select_fusion.5
  81.4 22.6 %collective-permute-done.8 = bf16[256,2048]{1,0:T(8,128)(2,1)} collective-permute-done((bf16[256,2048]{1,0:T(8,128)(2,1)}, bf16[256,2048]{1,0:T(8,128)(2,1)}, u32[]{:S(2)}, u32[]{:S(2)}) %collective-permute-start.8) | collective-permute-done | bytes 1048608 | tf_op jit(solution)/shard_map/ppermute | solution.py:108
  104.0 4.7 maximum_select_fusion.3
  117.3 4.0 all-to-all-start
  121.5 80.5 %all-to-all-done = f32[2,32,32]{1,0,2:T(2,128)} async-done(((f32[2,32,32]{1,0,2:T(2,128)}), f32[2,32,32]{1,0,2:T(2,128)}, u32[]{:S(2)}, u32[]{:S(2)}) %all-to-all-start) | async-done | bytes 8224 | tf_op jit(solution)/shard_map/all_to_all | solution.py:88
  204.9 9.4 %fusion.2 = f32[1024,768]{1,0:T(8,128)} fusion(bf16[1,2048,768]{2,1,0:T(8,128)(2,1)} %param.24, bf16[512,2048]{1,0:T(8,128)(2,1)} %collective-permute-done.9, bf16[512,2048]{1,0:T(8,128)(2,1)} %maximum_select_fusion.3, pred[]{:T(512)S(6)} %eq.60), kind=kOutput, calls=%fused_computation.6 | convolution fusion | flops 3240099840 | bytes 10485761 | tf_op jit(solution)/shard_map/dot_general | solution.py:64
  214.4 14.6 %multiply_convert_fusion = bf16[1024,2048]{1,0:T(8,128)(2,1)} fusion(f32[1024]{0:T(1024)} %mul.109, bf16[1,768,2048]{2,1,0:T(8,128)(2,1)S(1)} %copy-done, f32[1024,768]{1,0:T(8,128)} %fusion.2, bf16[1,2048,768]{2,1,0:T(8,128)(2,1)} %param.23, bf16[512,2048]{1,0:T(8,128)(2,1)} %collective-permute-done.9, bf16[512,2048]{1,0:T(8,128)(2,1)} %maximum_select_fusion.3, ...), kind=kOutput, calls=%fused_computation | convolution fusion | flops 6474432512 | bytes 17829888 | tf_op jit(solution)/shard_map/dot_general | solution.py:66
  231.3 10.6 %collective-permute-done.1 = bf16[64,2048]{1,0:T(8,128)(2,1)S(1)} collective-permute-done((bf16[64,2048]{1,0:T(8,128)(2,1)S(1)}, bf16[64,2048]{1,0:T(8,128)(2,1)S(1)}, u32[]{:S(2)}, u32[]{:S(2)}) %collective-permute-start.1) | collective-permute-done | bytes 262176 | tf_op jit(solution)/shard_map/ppermute | solution.py:108
  242.1 13.6 %collective-permute-done.2 = bf16[128,2048]{1,0:T(8,128)(2,1)S(1)} collective-permute-done((bf16[128,2048]{1,0:T(8,128)(2,1)S(1)}, bf16[128,2048]{1,0:T(8,128)(2,1)S(1)}, u32[]{:S(2)}, u32[]{:S(2)}) %collective-permute-start.2) | collective-permute-done | bytes 524320 | tf_op jit(solution)/shard_map/ppermute | solution.py:108
  257.2 26.3 %collective-permute-done.3 = bf16[256,2048]{1,0:T(8,128)(2,1)S(1)} collective-permute-done((bf16[256,2048]{1,0:T(8,128)(2,1)S(1)}, bf16[256,2048]{1,0:T(8,128)(2,1)S(1)}, u32[]{:S(2)}, u32[]{:S(2)}) %collective-permute-start.3) | collective-permute-done | bytes 1048608 | tf_op jit(solution)/shard_map/ppermute | solution.py:108
  283.5 2.5 maximum_select_fusion.2
  286.0 4.9 collective-permute-start.4
  291.0 97.9 %collective-permute-done.4 = bf16[512,2048]{1,0:T(8,128)(2,1)} collective-permute-done((bf16[512,2048]{1,0:T(8,128)(2,1)}, bf16[512,2048]{1,0:T(8,128)(2,1)}, u32[]{:S(2)}, u32[]{:S(2)}) %collective-permute-start.4) | collective-permute-done | bytes 2097184 | tf_op jit(solution)/shard_map/ppermute | solution.py:108
  388.9 9.6 %fusion.4 = f32[1024,768]{1,0:T(8,128)} fusion(bf16[1,2048,768]{2,1,0:T(8,128)(2,1)} %param.24, bf16[512,2048]{1,0:T(8,128)(2,1)} %collective-permute-done.4, bf16[512,2048]{1,0:T(8,128)(2,1)} %maximum_select_fusion.2, pred[]{:T(512)S(6)} %eq.60), kind=kOutput, calls=%fused_computation.8 | convolution fusion | flops 3240099840 | bytes 10485761 | tf_op jit(solution)/shard_map/dot_general | solution.py:64
  398.5 14.6 %multiply_convert_fusion.1 = bf16[1024,2048]{1,0:T(8,128)(2,1)} fusion(f32[1024]{0:T(1024)S(1)} %mul.96, bf16[1,768,2048]{2,1,0:T(8,128)(2,1)S(1)} %copy-done, f32[1024,768]{1,0:T(8,128)} %fusion.4, bf16[1,2048,768]{2,1,0:T(8,128)(2,1)} %param.23, bf16[512,2048]{1,0:T(8,128)(2,1)} %collective-permute-done.4, bf16[512,2048]{1,0:T(8,128)(2,1)} %maximum_select_fusion.2, ...), kind=kOutput, calls=%fused_computation.1 | convolution fusion | flops 6474432512 | bytes 17829888 | tf_op jit(solution)/shard_map/dot_general | solution.py:66
  413.8 141.4 %reduce-scatter.3.cloned.1.call-done = bf16[32,2048]{1,0:T(8,128)(2,1)} async-done(((bf16[1024,2048]{1,0:T(8,128)(2,1)}), bf16[32,2048]{1,0:T(8,128)(2,1)}) %reduce-scatter.3.cloned.1.call-update) | async-done | bytes 131088 | tf_op jit(solution)/shard_map/reduce_scatter | solution.py:115
  (93 shorter events, 54.3 us)
Async XLA Ops:
  6.5 207.8 %copy-start = (bf16[1,768,2048]{2,1,0:T(8,128)(2,1)S(1)}, bf16[1,768,2048]{2,1,0:T(8,128)(2,1)}, u32[]{:S(2)}) copy-start(bf16[1,768,2048]{2,1,0:T(8,128)(2,1)} %param.25) | copy-start | bytes 9437188
  21.7 8.5 %copy-start.7 = (f32[32,2,8]{2,1,0:T(2,128)}, f32[32,2,8]{2,1,0:T(2,128)S(1)}, u32[]{:S(2)}) copy-start(f32[32,2,8]{2,1,0:T(2,128)S(1)} %copy.60) | copy-start | bytes 6148
  43.6 1.9 copy-start.4
  43.6 1.9 copy-start.5
  43.6 1.9 copy-start.9
  45.4 1.3 copy-start.2
  45.4 1.0 copy-start.1
  45.5 1.3 copy-start.10
  45.9 1.7 copy-start.3
  47.6 1.8 collective-permute-start.5
  51.3 9.8 %collective-permute-start.6 = (bf16[64,2048]{1,0:T(8,128)(2,1)}, bf16[64,2048]{1,0:T(8,128)(2,1)}, u32[]{:S(2)}, u32[]{:S(2)}) collective-permute-start(bf16[64,2048]{1,0:T(8,128)(2,1)} %maximum_select_fusion.15), channel_id=1, source_target_pairs={{0,2},{1,3},{2,0},{3,1},{4,6},{5,7},{6,4},{7,5},{8,10},{9,11},{10,... | collective-permute-start | bytes 786440 | tf_op jit(solution)/shard_map/ppermute | solution.py:108
  63.2 13.8 %collective-permute-start.7 = (bf16[128,2048]{1,0:T(8,128)(2,1)}, bf16[128,2048]{1,0:T(8,128)(2,1)}, u32[]{:S(2)}, u32[]{:S(2)}) collective-permute-start(bf16[128,2048]{1,0:T(8,128)(2,1)} %maximum_select_fusion.13), channel_id=1, source_target_pairs={{0,4},{1,5},{2,6},{3,7},{4,0},{5,1},{6,2},{7,3},{8,12},{9,13},{10,... | collective-permute-start | bytes 1572872 | tf_op jit(solution)/shard_map/ppermute | solution.py:108
  65.0 45.9 %copy-start.8 = (f32[2,32,8]{1,2,0:T(8,128)S(1)}, f32[2,32,8]{1,2,0:T(8,128)}, u32[]{:S(2)}) copy-start(f32[2,32,8]{1,2,0:T(8,128)} %param.21) | copy-start | bytes 6148
  79.9 24.1 %collective-permute-start.8 = (bf16[256,2048]{1,0:T(8,128)(2,1)}, bf16[256,2048]{1,0:T(8,128)(2,1)}, u32[]{:S(2)}, u32[]{:S(2)}) collective-permute-start(bf16[256,2048]{1,0:T(8,128)(2,1)} %maximum_select_fusion.5), channel_id=1, source_target_pairs={{0,8},{1,9},{2,10},{3,11},{4,12},{5,13},{6,14},{7,15},{8,0},{9,1},... | collective-permute-start | bytes 3145736 | tf_op jit(solution)/shard_map/ppermute | solution.py:108
  108.7 96.2 %collective-permute-start.9 = (bf16[512,2048]{1,0:T(8,128)(2,1)}, bf16[512,2048]{1,0:T(8,128)(2,1)}, u32[]{:S(2)}, u32[]{:S(2)}) collective-permute-start(bf16[512,2048]{1,0:T(8,128)(2,1)} %maximum_select_fusion.3), channel_id=1, source_target_pairs={{0,16},{1,17},{2,18},{3,19},{4,20},{5,21},{6,22},{7,23},{8,24},{9,... | collective-permute-start | bytes 6291464 | tf_op jit(solution)/shard_map/ppermute | solution.py:108
  117.3 84.7 %all-to-all-start = ((f32[2,32,32]{1,0,2:T(2,128)}), f32[2,32,32]{1,0,2:T(2,128)}, u32[]{:S(2)}, u32[]{:S(2)}) async-start(f32[2,32,32]{1,0,2:T(2,128)} %copy.57), calls=%async_computation | async-start | bytes 65536 | tf_op jit(solution)/shard_map/all_to_all | solution.py:88
  121.2 292.6 %reduce-scatter.5.cloned.1.call-start = ((), (), s32[]{:S(2)}) async-start(), calls=%async_computation.4 | async-start | bytes 4325376 | tf_op jit(solution)/shard_map/reduce_scatter | solution.py:115
  229.0 326.2 %reduce-scatter.3.cloned.1.call-start = ((), (), s32[]{:S(2)}) async-start(), calls=%async_computation.3 | async-start | bytes 4325376 | tf_op jit(solution)/shard_map/reduce_scatter | solution.py:115
  229.2 1.4 collective-permute-start
  230.7 11.2 %collective-permute-start.1 = (bf16[64,2048]{1,0:T(8,128)(2,1)S(1)}, bf16[64,2048]{1,0:T(8,128)(2,1)S(1)}, u32[]{:S(2)}, u32[]{:S(2)}) collective-permute-start(bf16[64,2048]{1,0:T(8,128)(2,1)S(1)} %maximum_select_fusion.14), channel_id=1, source_target_pairs={{0,2},{1,3},{2,0},{3,1},{4,6},{5,7},{6,4},{7,5},{8,10},{9,11},{10,... | collective-permute-start | bytes 786440 | tf_op jit(solution)/shard_map/ppermute | solution.py:108
  242.0 13.7 %collective-permute-start.2 = (bf16[128,2048]{1,0:T(8,128)(2,1)S(1)}, bf16[128,2048]{1,0:T(8,128)(2,1)S(1)}, u32[]{:S(2)}, u32[]{:S(2)}) collective-permute-start(bf16[128,2048]{1,0:T(8,128)(2,1)S(1)} %maximum_select_fusion.12), channel_id=1, source_target_pairs={{0,4},{1,5},{2,6},{3,7},{4,0},{5,1},{6,2},{7,3},{8,12},{9,13},{10,... | collective-permute-start | bytes 1572872 | tf_op jit(solution)/shard_map/ppermute | solution.py:108
  256.0 27.5 %collective-permute-start.3 = (bf16[256,2048]{1,0:T(8,128)(2,1)S(1)}, bf16[256,2048]{1,0:T(8,128)(2,1)S(1)}, u32[]{:S(2)}, u32[]{:S(2)}) collective-permute-start(bf16[256,2048]{1,0:T(8,128)(2,1)S(1)} %maximum_select_fusion.4), channel_id=1, source_target_pairs={{0,8},{1,9},{2,10},{3,11},{4,12},{5,13},{6,14},{7,15},{8,0},{9,1},... | collective-permute-start | bytes 3145736 | tf_op jit(solution)/shard_map/ppermute | solution.py:108
  286.0 102.8 %collective-permute-start.4 = (bf16[512,2048]{1,0:T(8,128)(2,1)}, bf16[512,2048]{1,0:T(8,128)(2,1)}, u32[]{:S(2)}, u32[]{:S(2)}) collective-permute-start(bf16[512,2048]{1,0:T(8,128)(2,1)} %maximum_select_fusion.2), channel_id=1, source_target_pairs={{0,16},{1,17},{2,18},{3,19},{4,20},{5,21},{6,22},{7,23},{8,24},{9,... | collective-permute-start | bytes 6291464 | tf_op jit(solution)/shard_map/ppermute | solution.py:108
  413.1 0.7 copy-start.11
  (1 other events, 0.6 us)
Sparse Core Ops, SparseCore 0:
  229.1 148.1 reduce-scatter.4
  413.2 141.9 reduce-scatter.2
